TPU v7x, 512 devices: a whole 4x8x8 slice. The times are simulated.
512 devices in a mesh: dp: 128 (over z, y, core), tensor: 4 (over x).
Axes of the slice: x: 4, y: 8, z: 8, core: 2. Of those that a mesh axis runs over, the one named last changes fastest.
Arguments:
- hidden: bfloat16 [65536, 1024], P('dp', 'tensor'), may hold values from -24 to 24
- gain: float32 [1024], replicated, may hold values from 0.5 to 1.5
- head_weight: bfloat16 [1024, 25600], P(None, ('tensor', 'dp')), may hold values from -6 to 6
- targets: int32 [65536], P('dp'), may hold values from 0 to 25599
- row_count: int32 [128], P('dp'), may hold values from 64 to 512, as said below
- dest: int32 [65536], P('dp'), may hold values from 0 to 65535, as said below
Outputs:
- logprob: float32 [65536], P('dp')
- entropy: float32 [65536], P('dp')
Inputs may be any that keep to these rules, and one draw needn't show every extreme that they name: Each device's live slots are its first row_count ones; at least one device is full. dest is a permutation. Slot results of device s go to device dest // 512; every device sends exactly 4 results to every device, those from device s fill positions s * 4 to (s + 1) * 4 - 1 of the receiver's block, in the order of their position in the sender's slots sorted by destination.
All inputs are finite; a program needn't handle non-finite values.
Results may differ from a plain program's by a relative error of at most 0.0062.
Values may be sent and summed in bfloat16 or wider, within the bound.
A program may use at most 128 MiB of HBM per device.

v0:
```python
import jax
import jax.numpy as jnp
from jax import lax
from jax.sharding import PartitionSpec as P


def body(hidden, gain, head_weight, targets, row_count, dest):
    rows = hidden.shape[0]
    whole = lax.all_gather(hidden, "tensor", axis=1, tiled=True)
    wide = whole.astype(jnp.float32)
    power = jnp.mean(wide * wide, axis=1, keepdims=True)
    normed = (wide * lax.rsqrt(power + 1e-06) * gain).astype(jnp.bfloat16)
    shard_width = head_weight.shape[1] * lax.axis_size("dp")
    target_local = targets - lax.axis_index("tensor") * shard_width
    count = row_count[0]
    start_state = (
        jnp.full((rows,), -1e30, jnp.float32),
        jnp.zeros((rows,), jnp.float32),
        jnp.zeros((rows,), jnp.float32),
        jnp.zeros((rows,), jnp.float32),
    )
    block = min(256, rows)
    piece = lax.all_gather(head_weight, "dp", axis=1, tiled=True)
    nblocks = rows // block
    column_ids = jnp.arange(piece.shape[1], dtype=jnp.int32)

    def compute(index, state):
        first = index * block
        part_rows = lax.dynamic_slice_in_dim(normed, first, block, 0)
        logits = jnp.dot(part_rows, piece, preferred_element_type=jnp.float32)
        wanted = lax.dynamic_slice_in_dim(target_local, first, block, 0)
        old_top, old_mass, old_moment, old_pick = [
            lax.dynamic_slice_in_dim(item, first, block, 0) for item in state
        ]
        new_top = jnp.maximum(old_top, jnp.max(logits, axis=1))
        factor = jnp.exp(old_top - new_top)
        weights = jnp.exp(logits - new_top[:, None])
        new_mass = old_mass * factor + jnp.sum(weights, axis=1)
        new_moment = old_moment * factor + jnp.sum(weights * logits, axis=1)
        hit = column_ids[None, :] == wanted[:, None]
        new_pick = old_pick + jnp.sum(jnp.where(hit, logits, 0.0), axis=1)
        fresh = (new_top, new_mass, new_moment, new_pick)
        return tuple(
            (
                lax.dynamic_update_slice_in_dim(item, value, first, 0)
                for item, value in zip(state, fresh)
            )
        )

    top, mass, moment, picked = lax.fori_loop(0, nblocks, compute, start_state)
    global_top = lax.pmax(top, "tensor")
    factor = jnp.exp(top - global_top)
    mass, moment, picked = lax.psum((mass * factor, moment * factor, picked), "tensor")
    top = global_top
    live = jnp.arange(rows, dtype=jnp.int32) < count
    safe_mass = jnp.where(live, mass, 1.0)
    lse = top + jnp.log(safe_mass)
    value_lp = jnp.where(live, picked - lse, 0.0)
    value_ent = jnp.where(live, lse - moment / safe_mass, 0.0)
    values = jnp.stack([value_lp, value_ent])
    all_values, all_dest = (
        lax.all_gather(values, "dp", axis=1, tiled=True),
        lax.all_gather(dest, "dp", axis=0, tiled=True),
    )
    local = all_dest - lax.axis_index("dp") * rows
    local = jnp.where((local >= 0) & (local < rows), local, rows)
    result = jnp.zeros((2, rows), jnp.float32).at[:, local].set(all_values, mode="drop")
    return (result[0], result[1])


def solution(mesh):
    in_specs = (P("dp", "tensor"), P(), P(None, ("tensor", "dp")), P("dp"), P("dp"), P("dp"))
    out_specs = (P("dp"), P("dp"))
    return jax.shard_map(body, mesh=mesh, in_specs=in_specs, out_specs=out_specs, check_vma=False)
```

profile of v0, /device:TPU:1, one launch (start us, length us, event | category | flops | bytes accessed | tf_op | source)
XLA Modules:
  0.0 450.5 jit_solution(8561791773616338633)
XLA Ops:
  7.2 0.0 all-gather.5.cloned.1.call-start
  7.2 0.7 all-gather.5.cloned.1.call-update
  7.9 0.0 all-gather.7.cloned.1.call-start
  7.9 0.7 all-gather.7.cloned.1.call-update
  9.3 58.8 %all-gather = s32[128,1,512]{2,1,0:T(1,128)S(1)} all-gather(s32[1,1,512]{2,1,0:T(1,128)} %bitcast.23), channel_id=1, replica_groups=mesh['dp'=128,'tensor'=4] {'dp'}, dimensions={0}, use_global_device_ids=true | all-gather | bytes 264192 | tf_op jit(solution)/shard_map/all_gather | solution.py:63
  68.1 0.7 broadcast_subtract_fusion.1
  68.8 0.1 compare_select_fusion
  68.8 0.0 all-gather.5.cloned.1.call-done
  68.9 1.5 fusion.6
  70.4 1.5 fusion.8
  71.9 74.6 %all-gather.7.cloned.1.call-done = bf16[128,50,1024]{2,1,0:T(8,128)(2,1)} async-done(((bf16[1,50,1024]{2,1,0:T(8,128)(2,1)}), bf16[128,50,1024]{2,1,0:T(8,128)(2,1)}) %all-gather.7.cloned.1.call-update) | async-done | bytes 13107216 | tf_op jit(solution)/shard_map/all_gather | solution.py:23
  146.6 16.9 %reshape.28 = bf16[6400,1024]{1,0:T(8,128)(2,1)} reshape(bf16[128,50,1024]{2,1,0:T(8,128)(2,1)} %all-gather.7.cloned.1.call-done) | data formatting | bytes 26214400
  163.4 16.5 %copy.11 = bf16[1024,6400]{1,0:T(8,128)(2,1)} copy(bf16[1024,6400]{0,1:T(8,128)(2,1)} %bitcast.16) | data formatting | bytes 26214400
  180.0 19.7 %while.20 = (s32[]{:T(128)}, f32[512]{0:T(512)S(1)}, f32[512]{0:T(512)S(1)}, f32[512]{0:T(512)S(1)}, f32[512]{0:T(512)S(1)}, /*index=5*/bf16[512,1024]{1,0:T(8,1...) while((s32[]{:T(128)}, f32[512]{0:T(512)S(1)}, ...), condition=%wide.region_6.7_spmd.clone, body=%wide.region_1.6_spmd.clone.sunk | while | flops 3368551168 | bytes 26770612 | solution.py:50
  180.0 6.9 %fusion.21 = (f32[256]{0:T(256)S(1)}, f32[256,6400]{1,0:T(8,128)S(1)}) fusion(bf16[1024,6400]{1,0:T(8,128)(2,1)} %get-tuple-element.331, bf16[512,1024]{1,0:T(8,128)(2,1)S(1)} %get-tuple-element.330, s32[]{:T(128)S(6)} %select_n.63), kind=kOutput, calls=%fused_computation.38.clone.1 | convolution fusion | flops 3357081344 | bytes 20186116 | tf_op jit(solution)/shard_map/while/body/eval_jaxpr/dot_general | solution.py:30
  186.9 0.2 fusion.22
  187.1 0.1 dynamic_slice.69
  187.2 2.4 multiply_reduce_fusion.2
  189.6 0.2 add_dynamic-update-slice_fusion.4
  189.8 6.9 %fusion.21 = (f32[256]{0:T(256)S(1)}, f32[256,6400]{1,0:T(8,128)S(1)}) fusion(bf16[1024,6400]{1,0:T(8,128)(2,1)} %get-tuple-element.331, bf16[512,1024]{1,0:T(8,128)(2,1)S(1)} %get-tuple-element.330, s32[]{:T(128)S(6)} %select_n.63), kind=kOutput, calls=%fused_computation.38.clone.1 | convolution fusion | flops 3357081344 | bytes 20186116 | tf_op jit(solution)/shard_map/while/body/eval_jaxpr/dot_general | solution.py:30
  196.7 0.2 fusion.22
  196.9 0.1 dynamic_slice.69
  197.0 2.4 multiply_reduce_fusion.2
  199.4 0.2 add_dynamic-update-slice_fusion.4
  199.6 8.4 %pmax.7 = f32[512]{0:T(512)S(1)} all-reduce(f32[512]{0:T(512)S(1)} %get-tuple-element.160), channel_id=1, replica_groups=mesh['dp'=128,'tensor'=4] {'tensor'}, use_global_device_ids=true, to_apply=%region_8.9 | all-reduce | flops 512 | bytes 4096 | tf_op jit(solution)/shard_map/pmax | solution.py:51
  208.0 6.1 %all-reduce = (f32[512]{0:T(512)S(1)}, f32[512]{0:T(512)S(1)}, f32[512]{0:T(512)S(1)}) all-reduce(f32[512]{0:T(512)S(1)} %get-tuple-element.231, f32[512]{0:T(512)S(1)} %get-tuple-element.230, f32[512]{0:T(512)S(1)} %get-tuple-element.159), channel_id=1, replica_groups=mesh['dp'=128,'tensor'=4] {'tensor'}, use_global_device_ids=true, to_apply=%region_10.11 | all-reduce | flops 1536 | bytes 12288 | tf_op jit(solution)/shard_map/psum | solution.py:53
  214.2 53.4 %all_gather.15 = f32[2,65536]{1,0:T(2,128)S(1)} all-gather(f32[2,512]{1,0:T(2,128)S(1)} %pad_maximum_fusion), channel_id=1, replica_groups=mesh['dp'=128,'tensor'=4] {'dp'}, dimensions={1}, use_global_device_ids=true | all-gather | bytes 528384 | tf_op jit(solution)/shard_map/all_gather | solution.py:62
  267.5 15.6 %copy.12 = f32[65536,2]{1,0:T(8,128)} copy(f32[65536,2]{0,1:T(2,128)S(1)} %bitcast.17) | data formatting | bytes 1048576 | tf_op jit(solution)/shard_map/all_gather | solution.py:62
  283.1 159.6 %scatter_custom_fusion = f32[2,512]{0,1:T(8,128)S(1)} fusion(s32[65536]{0:T(1024)S(1)} %compare_select_fusion, f32[65536,2]{1,0:T(8,128)} %copy.12, f32[]{:T(128)} %constant.59.clone.1), kind=kCustom, calls=%fused_computation.24 | custom fusion | bytes 4608 | tf_op jit(solution)/shard_map/scatter | solution.py:67
  442.8 0.9 slice_reduce_fusion
  (13 shorter events, 0.1 us)
Async XLA Ops:
  7.2 61.7 %all-gather.5.cloned.1.call-start = ((), (), s32[]{:S(2)}) async-start(), calls=%async_computation | async-start | bytes 1310720 | tf_op jit(solution)/shard_map/all_gather | solution.py:9
  7.9 138.7 %all-gather.7.cloned.1.call-start = ((), (), s32[]{:S(2)}) async-start(), calls=%async_computation.1 | async-start | bytes 14794752 | tf_op jit(solution)/shard_map/all_gather | solution.py:23
Sparse Core Ops, SparseCore 0:
  10.1 34.7 all-gather.4
  47.9 98.5 all-gather.6
where the time goes:
time: 452 us; the launch traced here: 451 us
  local copies, waits for them, and re-layouts  210 us (46%)
  blocking collectives  127 us (28%)
  waiting for transfers between devices  76 us (17%)
  between operations  14.8 us (3%)
  matrix products  13.8 us (3%)
  other arithmetic  9.42 us (2%)
    scatter x1, local copies, waits for them, and re-layouts, body(): jnp.zeros((2, rows), jnp.float32).at[:, local].set(all_values, mode='drop')  160 us
    all_gather x1, waiting for transfers between devices, body(): piece = lax.all_gather(head_weight, 'dp', axis=1, tiled=True)  74.6 us
    all_gather x1, blocking collectives, body(): lax.all_gather(dest, 'dp', axis=0, tiled=True)  58.8 us
    all_gather x1, blocking collectives, body(): lax.all_gather(values, 'dp', axis=1, tiled=True)  53.4 us
    unnamed x2, local copies, waits for them, and re-layouts  33.4 us
    all_gather x1, local copies, waits for them, and re-layouts, body(): lax.all_gather(values, 'dp', axis=1, tiled=True)  15.6 us
    dot_general x2, matrix products, compute(): logits = jnp.dot(part_rows, piece, preferred_element_type=jnp.float32)  13.8 us
  transfers between devices with their start and end apart: 2, of which 1 were waited for; matrix products, arithmetic and copies ran while one was open for 1% of the time, Pallas kernels for 0%

commit v1 on v0

v1 whole, which is shorter than its diff:
```python
import jax
import jax.numpy as jnp
from jax import lax
from jax.sharding import Mesh, PartitionSpec as P


def stats_of(logits_t, wanted):
    top = jnp.max(logits_t, axis=0)
    weights = jnp.exp(logits_t - top[None, :])
    mass = jnp.sum(weights, axis=0)
    moment = jnp.sum(weights * logits_t, axis=0)
    ids = lax.broadcasted_iota(jnp.int32, logits_t.shape, 0)
    picked = jnp.sum(jnp.where(ids == wanted[None, :], logits_t, 0.0), axis=0)
    return jnp.stack([top, mass, moment, picked])


def merge(parts):
    top = jnp.max(parts[:, 0], axis=0)
    factor = jnp.exp(parts[:, 0] - top[None])
    mass = jnp.sum(parts[:, 1] * factor, axis=0)
    moment = jnp.sum(parts[:, 2] * factor, axis=0)
    return top, mass, moment, jnp.sum(parts[:, 3], axis=0)


def body(hidden, gain, head_weight, targets, row_count, dest):
    rows = hidden.shape[0]
    cols = head_weight.shape[1]
    padded = -(-cols // 8) * 8
    groups = lax.axis_size("zy") * 2
    tensors = lax.axis_size("tensor")
    core = lax.axis_index("core")
    mine = lax.axis_index("tensor")
    swap = [(0, 1), (1, 0)]
    spread = jnp.pad(head_weight.T, ((0, padded - cols), (0, 0)))
    piece = lax.all_gather(spread, "zy", axis=0, tiled=True)
    shards = [hidden]
    for step in range(1, tensors):
        shards.append(lax.ppermute(hidden, "tensor", [((i + step) % tensors, i) for i in range(tensors)]))
    own = jnp.stack(shards)
    other = lax.ppermute(own, "core", swap)
    both = jnp.concatenate([own, other], axis=1).astype(jnp.float32)
    power = jnp.sum(both * both, axis=(0, 2)) / (tensors * hidden.shape[1])
    scale = lax.rsqrt(power + 1e-06)
    gains = jnp.roll(gain.reshape(tensors, -1), -mine, axis=0)
    turned = (both * scale[None, :, None] * gains[:, None, :]).astype(jnp.bfloat16)
    ordered = jnp.roll(turned, mine, axis=0)
    normed = jnp.moveaxis(ordered, 0, 1).reshape(2 * rows, -1)
    wanted = jnp.concatenate([targets, lax.ppermute(targets, "core", swap)])
    local = wanted - mine * (cols * groups)
    device = local // cols
    ok = (local >= 0) & (device < groups) & (device % 2 == core)
    slot = jnp.where(ok, (device // 2) * padded + local % cols, -1)
    logits = lax.dot_general(piece, normed, (((1,), (1,)), ((), ())), preferred_element_type=jnp.float32)
    ids = lax.broadcasted_iota(jnp.int32, logits.shape, 0)
    logits = jnp.where(ids % padded < cols, logits, -1e30)
    stats = stats_of(logits, slot)
    theirs = lax.ppermute(stats[:, rows:], "core", swap)
    pair = jnp.stack(merge(jnp.stack([stats[:, :rows], theirs])))
    top, mass, moment, picked = merge(lax.all_gather(pair, "tensor", axis=0))
    live = jnp.arange(rows, dtype=jnp.int32) < row_count[0]
    lse = top + jnp.log(mass)
    value_lp = jnp.where(live, picked - lse, 0.0)
    value_ent = jnp.where(live, lse - moment / mass, 0.0)
    share = rows // groups
    rank = (dest // rows) * share + dest % share
    hit = lax.broadcasted_iota(jnp.int32, (rows, rows), 0) == rank[None, :]
    sent = [jnp.sum(jnp.where(hit, v[None, :], 0.0), axis=1).reshape(groups, share) for v in (value_lp, value_ent)]
    got = lax.all_to_all(jnp.concatenate(sent, axis=1), ("zy", "core"), 0, 0, tiled=True)
    return got[:, :share].reshape(rows), got[:, share:].reshape(rows)


def solution(mesh):
    dp, tensor = mesh.devices.shape
    fine = Mesh(mesh.devices.reshape(dp // 2, 2, tensor), ("zy", "core", "tensor"))
    group = ("zy", "core")
    in_specs = (P(group, "tensor"), P(), P(None, ("tensor", "zy", "core")), P(group), P(group), P(group))
    return jax.shard_map(body, mesh=fine, in_specs=in_specs, out_specs=(P(group), P(group)), check_vma=False)
```

time: 452 us -> 173 us (0.38)
  local copies, waits for them, and re-layouts: 210 us -> 5.03 us
  blocking collectives: 127 us -> 33.6 us
  starting transfers between devices: 0.08 us -> 21.4 us
    scatter x1 -> x0, local copies, waits for them, and re-layouts: 160 us -> none  [body(): jnp.zeros((2, rows), jnp.float32).at[:, local].set(all_values, mode='drop')]
    all_gather x2 -> x1, blocking collectives: 112 us -> 9.34 us  [body(): top, mass, moment, picked = merge(lax.all_gather(pair, 'tensor', axis=0))]
    unnamed x2 -> x3, local copies, waits for them, and re-layouts: 33.4 us -> 1.1 us
    all_to_all x0 -> x1, blocking collectives: none -> 24.2 us  [body(): lax.all_to_all(jnp.concatenate(sent, axis=1), ('zy', 'core'), 0, 0, tiled...]
    ppermute x0 -> x6, starting transfers between devices: none -> 21.4 us  [the longest x3 10.1 us: body(): lax.ppermute(hidden, 'tensor', [((i + step) % tensors, i) for i in range(...]
    all_gather x1 -> x0, local copies, waits for them, and re-layouts: 15.6 us -> none  [body(): lax.all_gather(values, 'dp', axis=1, tiled=True)]
    ppermute x0 -> x6, waiting for transfers between devices: none -> 9.08 us  [the longest x3 8.43 us: body(): lax.ppermute(hidden, 'tensor', [((i + step) % tensors, i) for i in range(...]
    pmax x1 -> x0, blocking collectives: 8.41 us -> none  [body(): global_top = lax.pmax(top, 'tensor')]
  transfers between devices with their start and end apart: 2 -> 7, of which waited for: 1 -> 5; matrix products, arithmetic and copies ran while one was open for 1% -> 3% of each run, Pallas kernels for 0% -> 0%
where the time goes in v1:
time: 173 us
  waiting for transfers between devices  79 us (46%)
  blocking collectives  33.6 us (19%)
  starting transfers between devices  21.4 us (12%)
  between operations  14.9 us (9%)
  matrix products  10.5 us (6%)
  other arithmetic  8.21 us (5%)
  local copies, waits for them, and re-layouts  5.03 us (3%)
    all_gather x1, waiting for transfers between devices, body(): piece = lax.all_gather(spread, 'zy', axis=0, tiled=True)  69.9 us
    all_to_all x1, blocking collectives, body(): lax.all_to_all(jnp.concatenate(sent, axis=1), ('zy', 'core'), 0, 0, tiled...  24.2 us
    dot_general x1, matrix products, body(): lax.dot_general(piece, normed, (((1,), (1,)), ((), ())), preferred_elemen...  10.5 us
    ppermute x3, starting transfers between devices, body(): lax.ppermute(hidden, 'tensor', [((i + step) % tensors, i) for i in range(...  10.1 us
    all_gather x1, blocking collectives, body(): top, mass, moment, picked = merge(lax.all_gather(pair, 'tensor', axis=0))  9.34 us
    ppermute x3, waiting for transfers between devices, body(): lax.ppermute(hidden, 'tensor', [((i + step) % tensors, i) for i in range(...  8.43 us
    ppermute x1, starting transfers between devices, body(): other = lax.ppermute(own, 'core', swap)  6.25 us
    reduce_sum x1, other arithmetic, stats_of(): mass = jnp.sum(weights, axis=0)  4.82 us
  transfers between devices with their start and end apart: 7, of which 5 were waited for; matrix products, arithmetic and copies ran while one was open for 3% of the time, Pallas kernels for 0%

profile of v1, /device:TPU:1, one launch (start us, length us, event | category | flops | bytes accessed | tf_op | source)
XLA Modules:
  0.0 172.6 jit_solution(16111850264375092905)
XLA Ops:
  7.2 0.0 all-gather.4.cloned.1.call-start
  7.2 1.6 pad.4
  8.8 0.0 all-gather.4.cloned.1.call-update
  8.8 1.1 copy.31
  9.9 5.2 %collective-permute-start = (bf16[512,256]{0,1:T(8,128)(2,1)S(1)}, bf16[512,256]{0,1:T(8,128)(2,1)S(1)}, u32[]{:S(2)}, u32[]{:S(2)}) collective-permute-start(bf16[512,256]{0,1:T(8,128)(2,1)S(1)} %copy.31), channel_id=1, source_target_pairs={{1,0},{2,1},{3,2},{0,3},{5,4},{6,5},{7,6},{4,7},{9,8},{10,9},{11,1... | collective-permute-start | bytes 786440 | tf_op jit(solution)/shard_map/ppermute | solution.py:38
  15.1 2.4 %collective-permute-start.1 = (bf16[512,256]{0,1:T(8,128)(2,1)S(1)}, bf16[512,256]{0,1:T(8,128)(2,1)S(1)}, u32[]{:S(2)}, u32[]{:S(2)}) collective-permute-start(bf16[512,256]{0,1:T(8,128)(2,1)S(1)} %copy.31), channel_id=1, source_target_pairs={{2,0},{3,1},{0,2},{1,3},{6,4},{7,5},{4,6},{5,7},{10,8},{11,9},{8,1... | collective-permute-start | bytes 786440 | tf_op jit(solution)/shard_map/ppermute | solution.py:38
  17.5 2.5 %collective-permute-start.2 = (bf16[512,256]{0,1:T(8,128)(2,1)S(1)}, bf16[512,256]{0,1:T(8,128)(2,1)S(1)}, u32[]{:S(2)}, u32[]{:S(2)}) collective-permute-start(bf16[512,256]{0,1:T(8,128)(2,1)S(1)} %copy.31), channel_id=1, source_target_pairs={{3,0},{0,1},{1,2},{2,3},{7,4},{4,5},{5,6},{6,7},{11,8},{8,9},{9,10... | collective-permute-start | bytes 786440 | tf_op jit(solution)/shard_map/ppermute | solution.py:38
  20.1 0.0 collective-permute-done
  20.1 3.7 %collective-permute-done.1 = bf16[512,256]{0,1:T(8,128)(2,1)S(1)} collective-permute-done((bf16[512,256]{0,1:T(8,128)(2,1)S(1)}, bf16[512,256]{0,1:T(8,128)(2,1)S(1)}, u32[]{:S(2)}, u32[]{:S(2)}) %collective-permute-start.1) | collective-permute-done | bytes 262176 | tf_op jit(solution)/shard_map/ppermute | solution.py:38
  23.8 4.7 %collective-permute-done.2 = bf16[512,256]{0,1:T(8,128)(2,1)S(1)} collective-permute-done((bf16[512,256]{0,1:T(8,128)(2,1)S(1)}, bf16[512,256]{0,1:T(8,128)(2,1)S(1)}, u32[]{:S(2)}, u32[]{:S(2)}) %collective-permute-start.2) | collective-permute-done | bytes 262176 | tf_op jit(solution)/shard_map/ppermute | solution.py:38
  28.5 0.1 pad_maximum_fusion.1
  28.6 6.2 %collective-permute-start.3 = (bf16[4,512,256]{1,2,0:T(8,128)(2,1)S(1)}, bf16[4,512,256]{1,2,0:T(8,128)(2,1)S(1)}, u32[]{:S(2)}, u32[]{:S(2)}) collective-permute-start(bf16[4,512,256]{1,2,0:T(8,128)(2,1)S(1)} %pad_maximum_fusion.1), channel_id=1, source_target_pairs={{0,4},{4,0},{1,5},{5,1},{2,6},{6,2},{3,7},{7,3},{8,12},{12,8},{9,1... | collective-permute-start | bytes 3145736 | tf_op jit(solution)/shard_map/ppermute | solution.py:40
  34.9 1.9 %collective-permute-start.4 = (s32[512]{0:T(512)}, s32[512]{0:T(512)S(1)}, u32[]{:S(2)}, u32[]{:S(2)}) collective-permute-start(s32[512]{0:T(512)} %param.9), channel_id=1, source_target_pairs={{0,4},{4,0},{1,5},{5,1},{2,6},{6,2},{3,7},{7,3},{8,12},{12,8},{9,1... | collective-permute-start | bytes 6152 | tf_op jit(solution)/shard_map/ppermute | solution.py:48
  36.8 0.7 reshape.120
  37.6 0.5 collective-permute-done.4
  38.2 0.7 fusion.21
  38.9 0.0 collective-permute-done.3
  38.9 0.5 fusion.2
  39.4 0.6 fusion.4
  40.0 0.8 fusion.5
  40.8 69.9 %all-gather.4.cloned.1.call-done = bf16[3584,1024]{1,0:T(8,128)(2,1)} async-done(((bf16[56,1024]{1,0:T(8,128)(2,1)}), bf16[3584,1024]{1,0:T(8,128)(2,1)}) %all-gather.4.cloned.1.call-update) | async-done | bytes 7340048 | tf_op jit(solution)/shard_map/all_gather | solution.py:35
  110.7 10.5 %fusion.40 = (f32[1024]{0:T(1024)S(1)}, f32[3584,1024]{1,0:T(8,128)S(1)}) fusion(bf16[3584,1024]{1,0:T(8,128)(2,1)} %all-gather.4.cloned.1.call-done, bf16[1024,1024]{0,1:T(8,128)(2,1)S(1)} %bitcast.76, s32[3584]{0:T(1024)S(1)} %get-tuple-element.29, s32[3584]{0:T(1024)S(1)} %get-tuple-element.30, pred[3584]{0:T(1024)(128)(4,1)S(1)} %fusion.9), kind=kOutput, calls=%fused_computation.97 | convolution fusion | flops 7530871808 | bytes 24153600 | tf_op jit(solution)/shard_map/dot_general | solution.py:53
  121.1 0.0 copy-start
  121.1 4.8 %fusion = (f32[1024]{0:T(1024)S(1)}, f32[1024]{0:T(1024)S(1)}, f32[1024]{0:T(1024)S(1)}) fusion(f32[3584,1024]{1,0:T(8,128)S(1)} %get-tuple-element.28, f32[1024]{0:T(1024)S(1)} %get-tuple-element.27, s32[1024]{0:T(1024)S(1)} %fusion.21), kind=kLoop, calls=%fused_computation.4 | loop fusion | flops 25687040 | bytes 14700544 | tf_op jit(solution)/shard_map/reduce_sum | solution.py:10
  126.0 3.0 %collective-permute-start.5 = (f32[4,512]{1,0:T(4,128)S(1)}, f32[4,512]{1,0:T(4,128)S(1)}, u32[]{:S(2)}, u32[]{:S(2)}) collective-permute-start(f32[4,512]{1,0:T(4,128)S(1)} %get-tuple-element.24), channel_id=1, source_target_pairs={{0,4},{4,0},{1,5},{5,1},{2,6},{6,2},{3,7},{7,3},{8,12},{12,8},{9,1... | collective-permute-start | bytes 24584 | tf_op jit(solution)/shard_map/ppermute | solution.py:57
  129.1 0.0 copy-done
  129.8 0.1 collective-permute-done.5
  130.0 9.3 %all-gather.1 = f32[4,4,512]{2,1,0:T(4,128)S(1)} all-gather(f32[1,4,512]{2,1,0:T(4,128)S(1)} %maximum_bitcast_fusion), channel_id=2, replica_groups=mesh['zy'=64,'core'=2,'tensor'=4] {'tensor'}, dimensions={0}, use_global_device_ids=true | all-gather | bytes 40960 | tf_op jit(solution)/shard_map/all_gather | solution.py:59
  139.4 0.4 select_reduce_fusion.2
  139.8 0.1 reshape.122
  139.9 0.1 reshape.123
  140.0 0.1 pad_maximum_fusion.2
  140.1 24.2 %all_to_all.12 = f32[128,1,8]{2,1,0:T(1,128)S(1)} all-to-all(f32[128,1,8]{2,1,0:T(1,128)S(1)} %bitcast.78), channel_id=1, replica_groups=mesh['zy'=64,'core'=2,'tensor'=4] {'zy','core'}, dimensions={0} | all-to-all | bytes 8192 | tf_op jit(solution)/shard_map/all_to_all | solution.py:68
  164.3 0.1 fusion.38
  164.4 0.7 reshape.124
  165.1 0.7 reshape.125
  (15 shorter events, 0.3 us)
Async XLA Ops:
  7.2 103.5 %all-gather.4.cloned.1.call-start = ((), (), s32[]{:S(2)}) async-start(), calls=%async_computation.1 | async-start | bytes 7454720 | tf_op jit(solution)/shard_map/all_gather | solution.py:35
  9.9 10.2 %collective-permute-start = (bf16[512,256]{0,1:T(8,128)(2,1)S(1)}, bf16[512,256]{0,1:T(8,128)(2,1)S(1)}, u32[]{:S(2)}, u32[]{:S(2)}) collective-permute-start(bf16[512,256]{0,1:T(8,128)(2,1)S(1)} %copy.31), channel_id=1, source_target_pairs={{1,0},{2,1},{3,2},{0,3},{5,4},{6,5},{7,6},{4,7},{9,8},{10,9},{11,1... | collective-permute-start | bytes 786440 | tf_op jit(solution)/shard_map/ppermute | solution.py:38
  15.1 8.7 %collective-permute-start.1 = (bf16[512,256]{0,1:T(8,128)(2,1)S(1)}, bf16[512,256]{0,1:T(8,128)(2,1)S(1)}, u32[]{:S(2)}, u32[]{:S(2)}) collective-permute-start(bf16[512,256]{0,1:T(8,128)(2,1)S(1)} %copy.31), channel_id=1, source_target_pairs={{2,0},{3,1},{0,2},{1,3},{6,4},{7,5},{4,6},{5,7},{10,8},{11,9},{8,1... | collective-permute-start | bytes 786440 | tf_op jit(solution)/shard_map/ppermute | solution.py:38
  17.5 11.0 %collective-permute-start.2 = (bf16[512,256]{0,1:T(8,128)(2,1)S(1)}, bf16[512,256]{0,1:T(8,128)(2,1)S(1)}, u32[]{:S(2)}, u32[]{:S(2)}) collective-permute-start(bf16[512,256]{0,1:T(8,128)(2,1)S(1)} %copy.31), channel_id=1, source_target_pairs={{3,0},{0,1},{1,2},{2,3},{7,4},{4,5},{5,6},{6,7},{11,8},{8,9},{9,10... | collective-permute-start | bytes 786440 | tf_op jit(solution)/shard_map/ppermute | solution.py:38
  28.6 10.2 %collective-permute-start.3 = (bf16[4,512,256]{1,2,0:T(8,128)(2,1)S(1)}, bf16[4,512,256]{1,2,0:T(8,128)(2,1)S(1)}, u32[]{:S(2)}, u32[]{:S(2)}) collective-permute-start(bf16[4,512,256]{1,2,0:T(8,128)(2,1)S(1)} %pad_maximum_fusion.1), channel_id=1, source_target_pairs={{0,4},{4,0},{1,5},{5,1},{2,6},{6,2},{3,7},{7,3},{8,12},{12,8},{9,1... | collective-permute-start | bytes 3145736 | tf_op jit(solution)/shard_map/ppermute | solution.py:40
  34.9 3.3 %collective-permute-start.4 = (s32[512]{0:T(512)}, s32[512]{0:T(512)S(1)}, u32[]{:S(2)}, u32[]{:S(2)}) collective-permute-start(s32[512]{0:T(512)} %param.9), channel_id=1, source_target_pairs={{0,4},{4,0},{1,5},{5,1},{2,6},{6,2},{3,7},{7,3},{8,12},{12,8},{9,1... | collective-permute-start | bytes 6152 | tf_op jit(solution)/shard_map/ppermute | solution.py:48
  121.1 7.9 %copy-start = (s32[512]{0:T(512)S(1)}, s32[512]{0:T(512)}, u32[]{:S(2)}) copy-start(s32[512]{0:T(512)} %param.11) | copy-start | bytes 6148
  126.0 3.9 %collective-permute-start.5 = (f32[4,512]{1,0:T(4,128)S(1)}, f32[4,512]{1,0:T(4,128)S(1)}, u32[]{:S(2)}, u32[]{:S(2)}) collective-permute-start(f32[4,512]{1,0:T(4,128)S(1)} %get-tuple-element.24), channel_id=1, source_target_pairs={{0,4},{4,0},{1,5},{5,1},{2,6},{6,2},{3,7},{7,3},{8,12},{12,8},{9,1... | collective-permute-start | bytes 24584 | tf_op jit(solution)/shard_map/ppermute | solution.py:57
Sparse Core Ops, SparseCore 0:
  11.0 99.6 all-gather.3

commit v2 on v1

v2 whole, which is shorter than its diff:
```python
import functools

import jax
import jax.numpy as jnp
from jax import lax
from jax.experimental import pallas as pl
from jax.experimental.pallas import tpu as pltpu
from jax.sharding import Mesh, PartitionSpec as P

RING = 8
TENSORS = 4
MAIN = 48
CHUNK = 256
F32 = jnp.float32


def zigzag(i):
    return ((i + 1) >> 1) * (1 - 2 * (i & 1))


def head_kernel(main_hbm, rest_hbm, hid_hbm, code_hbm, gain_ref, out_ref,
                wbuf, lbuf, hbuf, cbuf, normed, wide_rest, rest, stats, packed, gath,
                w_recv, w_send, h_recv, h_send, c_sem, s_recv, s_send, local_sem):
    z, y = lax.axis_index("z"), lax.axis_index("y")
    core, x = lax.axis_index("core"), lax.axis_index("tensor")
    rows = hid_hbm.shape[1]
    feats = hid_hbm.shape[0]
    p = z + core * (y - z)
    q = y + core * (z - y)

    def wrap(v):
        return (v + 2 * RING) & (RING - 1)

    def at(pp, qq):
        return (pp + core * (qq - pp), qq + core * (pp - qq), core, x)

    def at_x(xx, cc):
        return (z, y, cc, (xx + 2 * TENSORS) & (TENSORS - 1))

    right1, left1 = at(wrap(p + 1), q), at(wrap(p - 1), q)
    right2, left2 = at(p, wrap(q + 1)), at(p, wrap(q - 1))
    partner = at_x(x, 1 - core)
    slot0 = q * RING + p

    locals_ = [
        pltpu.make_async_copy(main_hbm, wbuf.at[slot0], local_sem.at[0]),
        pltpu.make_async_copy(rest_hbm, lbuf.at[slot0], local_sem.at[1]),
        pltpu.make_async_copy(hid_hbm, hbuf.at[core, x], local_sem.at[2]),
        pltpu.make_async_copy(code_hbm, cbuf.at[core], local_sem.at[3]),
    ]
    for copy in locals_:
        copy.start()
    barrier = pltpu.get_barrier_semaphore()
    peers = [at_x(x + d, c) for d in range(TENSORS) for c in (core, 1 - core)][1:]
    for peer in [right1, left1, right2, left2] + peers:
        pl.semaphore_signal(barrier, inc=1, device_id=peer, device_id_type=pl.DeviceIdType.MESH)
    for copy in locals_:
        copy.wait()
    pl.semaphore_wait(barrier, 4 + len(peers))

    def block(slot, kind, target):
        return [
            pltpu.make_async_remote_copy(
                src_ref=buf.at[slot], dst_ref=buf.at[slot],
                send_sem=w_send.at[kind, n, slot], recv_sem=w_recv.at[n, slot],
                device_id=target, device_id_type=pl.DeviceIdType.MESH)
            for n, buf in enumerate((wbuf, lbuf))
        ]

    def start(slot, kind, target):
        for copy in block(slot, kind, target):
            copy.start()

    def arrive(slot):
        for copy in block(slot, 0, right1):
            copy.wait_recv()

    def sent(slot, kind):
        for copy in block(slot, kind, right1):
            copy.wait_send()

    def states(cc, xx, kind, target):
        xs = (xx + 2 * TENSORS) & (TENSORS - 1)
        return pltpu.make_async_remote_copy(
            src_ref=hbuf.at[cc, xs], dst_ref=hbuf.at[cc, xs],
            send_sem=h_send.at[kind, xs], recv_sem=h_recv.at[cc, xs],
            device_id=target, device_id_type=pl.DeviceIdType.MESH)

    codes = pltpu.make_async_remote_copy(
        src_ref=cbuf.at[core], dst_ref=cbuf.at[core], send_sem=c_sem.at[0], recv_sem=c_sem.at[1],
        device_id=partner, device_id_type=pl.DeviceIdType.MESH)
    way = 1 - 2 * core
    start(slot0, 0, right1)
    start(slot0, 1, left1)
    states(core, x, 0, at_x(x + 1, core)).start()
    states(core, x, 1, at_x(x - 1, core)).start()
    states(core, x, 3, partner).start()
    codes.start()
    start(slot0, 2, right2)
    start(slot0, 3, left2)

    def first(i):
        slot = q * RING + wrap(p + zigzag(i))
        arrive(slot)
        if i in (1, 3, 5):
            start(slot, 0, right1)
        if i in (2, 4):
            start(slot, 1, left1)
        start(slot, 2, right2)
        start(slot, 3, left2)

    for i in range(1, 4):
        first(i)
    for d in (-1, 1):
        states(core, x + d, 0, partner).wait_recv()
    states(core, x - way, 2, at_x(x + way, core)).start()
    for d in (-1, 1):
        states(core, x + d, 3, partner).start()
    for i in range(4, 8):
        first(i)

    def from_left(t, i, forward):
        slot = wrap(q - t) * RING + wrap(p + zigzag(i))
        arrive(slot)
        if forward:
            start(slot, 2, right2)

    def from_right(t, i, forward):
        slot = wrap(q + t) * RING + wrap(p + zigzag(i))
        arrive(slot)
        if forward:
            start(slot, 3, left2)

    def both(t, low, high):
        @pl.loop(low, high)
        def _(i):
            from_left(t, i, True)
            from_right(t, i, True)

    both(1, 0, 4)
    states(core, x + 2, 0, partner).wait_recv()
    states(core, x + 2, 3, partner).start()
    both(1, 4, 8)

    for d in range(TENSORS):
        states(1 - core, x + d, 0, partner).wait_recv()
    codes.wait_recv()
    for c in range(2):
        power = jnp.zeros((1, rows), F32)
        for d in range(TENSORS):
            part = hbuf[c, d].astype(F32)
            power += jnp.sum(part * part, axis=0, keepdims=True)
        scale = lax.rsqrt(power / (TENSORS * feats) + 1e-06)
        for d in range(TENSORS):
            span = pl.ds(d * feats, feats)
            part = hbuf[c, d].astype(F32) * scale * gain_ref[span, :]
            normed[span, pl.ds(c * rows, rows)] = part.astype(jnp.bfloat16)
    stats[0] = jnp.full(stats.shape[1:], -1e30, F32)
    for n in range(1, 4):
        stats[n] = jnp.zeros(stats.shape[1:], F32)
    mine = (x * 2 + core) * 4096
    per = rows // CHUNK

    def update(weights, count, base, r):
        cols = pl.ds(pl.multiple_of(r * CHUNK, CHUNK), CHUNK)
        logits = jnp.dot(weights, normed[:, cols], preferred_element_type=F32)
        cube = logits.reshape(count // 8, 8, CHUNK)
        half = r // per
        span = pl.ds(pl.multiple_of((r - half * per) * CHUNK, CHUNK), CHUNK)
        wanted = cbuf[half, :, span] - (mine + base)
        ids = lax.broadcasted_iota(jnp.int32, (count, CHUNK), 0)
        old = stats[0, :, cols]
        top = jnp.maximum(old, jnp.max(cube, axis=0))
        factor = jnp.exp(old - top)
        weight = jnp.exp(cube - top[None])
        stats[0, :, cols] = top
        stats[1, :, cols] = stats[1, :, cols] * factor + jnp.sum(weight, axis=0)
        stats[2, :, cols] = stats[2, :, cols] * factor + jnp.sum(weight * cube, axis=0)
        hit = jnp.where(ids == wanted, logits, 0.0).reshape(count // 8, 8, CHUNK)
        stats[3, :, cols] = stats[3, :, cols] + jnp.sum(hit, axis=0)

    chunks = 2 * per

    def unit(u):
        k = u // chunks
        r = u - k * chunks
        g = wrap(q + zigzag(k))
        weights = wbuf[pl.ds(pl.multiple_of(g * RING, RING), RING)].reshape(RING * MAIN, -1)
        update(weights, RING * MAIN, g * (RING * MAIN), r)

    @pl.loop(0, 8)
    def _(i):
        from_left(2, i, True)
        from_right(2, i, True)
        unit(i)

    @pl.loop(0, 4)
    def _(i):
        from_left(3, i, True)
        from_right(3, i, False)
        unit(8 + i)

    @pl.loop(4, 8)
    def _(i):
        from_left(3, i, False)
        from_right(3, i, True)
        unit(8 + i)

    @pl.loop(0, 4)
    def _(i):
        from_left(4, i, False)
        unit(16 + 2 * i)
        from_right(4, i + 4, False)
        unit(17 + 2 * i)

    @pl.loop(24, 32)
    def _(u):
        unit(u)

    total = RING * RING * 2
    wide_rest[...] = lbuf[...].astype(F32).reshape(total * 8, 128)
    for k in range(8):
        rest[:, pl.ds(k * 128, 128)] = wide_rest[pl.ds(k, total, stride=8), :].astype(jnp.bfloat16)

    @pl.loop(0, chunks)
    def _(r):
        update(rest[...], total, RING * RING * MAIN, r)

    top = jnp.max(stats[0], axis=0, keepdims=True)
    factor = jnp.exp(stats[0] - top)
    lines = [top] + [jnp.sum(stats[n] * factor, axis=0, keepdims=True) for n in (1, 2)]
    lines.append(jnp.sum(stats[3], axis=0, keepdims=True))
    for c in range(2):
        for n, line in enumerate(lines):
            packed[c, pl.ds(n, 1), :] = line[:, c * rows:(c + 1) * rows]
        packed[c, pl.ds(4, 4), :] = jnp.zeros((4, rows), F32)
    who = x * 2 + core

    def result(n, peer):
        return pltpu.make_async_remote_copy(
            src_ref=packed.at[peer[2]], dst_ref=gath.at[who],
            send_sem=s_send.at[n], recv_sem=s_recv.at[who],
            device_id=peer, device_id_type=pl.DeviceIdType.MESH)

    def result_from(n, peer):
        source = peer[3] * 2 + peer[2]
        return pltpu.make_async_remote_copy(
            src_ref=packed.at[core], dst_ref=gath.at[source],
            send_sem=s_send.at[n], recv_sem=s_recv.at[source],
            device_id=peer, device_id_type=pl.DeviceIdType.MESH)

    for n, peer in enumerate(peers):
        result(n, peer).start()
    own = pltpu.make_async_copy(packed.at[core], gath.at[who], local_sem.at[0])
    own.start()

    for t in range(4):
        sent(q * RING + wrap(p - t), 0)
    for t in range(3):
        sent(q * RING + wrap(p + t), 1)

    @pl.loop(0, 8)
    def _(i):
        pp = wrap(p + zigzag(i))
        for t in range(3):
            sent(wrap(q - t) * RING + pp, 2)
            sent(wrap(q + t) * RING + pp, 3)

    @pl.loop(0, 4)
    def _(i):
        sent(wrap(q - 3) * RING + wrap(p + zigzag(i)), 2)
        sent(wrap(q + 3) * RING + wrap(p + zigzag(i + 4)), 3)

    states(core, x, 0, partner).wait_send()
    states(core, x, 1, partner).wait_send()
    states(core, x - way, 2, partner).wait_send()
    for d in range(TENSORS):
        states(core, x + d, 3, partner).wait_send()
    codes.wait_send()
    own.wait()
    for n, peer in enumerate(peers):
        result_from(n, peer).wait_recv()
        result(n, peer).wait_send()
    out_ref[...] = gath[...]


def head(main, rest, hid, code, gain):
    rows, feats, slots = hid.shape[1], hid.shape[0], RING * RING
    depth = TENSORS * feats
    any_space = pl.BlockSpec(memory_space=pl.ANY)
    vmem = pl.BlockSpec(memory_space=pltpu.VMEM)
    dma = pltpu.SemaphoreType.DMA
    return pl.pallas_call(
        head_kernel,
        out_shape=jax.ShapeDtypeStruct((2 * TENSORS, 8, rows), F32),
        in_specs=[any_space] * 4 + [vmem],
        out_specs=vmem,
        scratch_shapes=[
            pltpu.VMEM((slots, MAIN, depth), jnp.bfloat16),
            pltpu.VMEM((slots, 16, 128), jnp.bfloat16),
            pltpu.VMEM((2, TENSORS, feats, rows), jnp.bfloat16),
            pltpu.VMEM((2, 1, rows), jnp.int32),
            pltpu.VMEM((depth, 2 * rows), jnp.bfloat16),
            pltpu.VMEM((slots * 16, 128), F32),
            pltpu.VMEM((slots * 2, depth), jnp.bfloat16),
            pltpu.VMEM((4, 8, 2 * rows), F32),
            pltpu.VMEM((2, 8, rows), F32),
            pltpu.VMEM((2 * TENSORS, 8, rows), F32),
            dma((2, slots)), dma((4, 2, slots)), dma((2, TENSORS)), dma((4, TENSORS)),
            dma((2,)), dma((2 * TENSORS,)), dma((2 * TENSORS,)), dma((4,)),
        ],
        compiler_params=pltpu.CompilerParams(
            collective_id=0, has_side_effects=True, vmem_limit_bytes=48 << 20),
    )(main, rest, hid, code, gain)


def body(hidden, gain, head_weight, targets, row_count, dest):
    rows = hidden.shape[0]
    cols = head_weight.shape[1]
    groups = 2 * RING * RING
    turned = head_weight.T
    rest = turned[MAIN:].reshape(16, 128)
    owner, column = targets // (cols * groups), targets % cols
    device = (targets // cols) % groups
    near, zy = device % 2, device // 2
    zi, yi = zy // RING, zy % RING
    slot = jnp.where(near == 0, yi * RING + zi, zi * RING + yi)
    index = jnp.where(column < MAIN, slot * MAIN + column, RING * RING * MAIN + slot * 2 + column - MAIN)
    code = ((owner * 2 + near) * 4096 + index).reshape(1, rows)
    parts = head(turned[:MAIN], rest, hidden.T, code, gain.reshape(-1, 1))
    top = jnp.max(parts[:, 0], axis=0)
    factor = jnp.exp(parts[:, 0] - top[None])
    mass = jnp.sum(parts[:, 1] * factor, axis=0)
    moment = jnp.sum(parts[:, 2] * factor, axis=0)
    picked = jnp.sum(parts[:, 3], axis=0)
    live = jnp.arange(rows, dtype=jnp.int32) < row_count[0]
    lse = top + jnp.log(mass)
    value_lp = jnp.where(live, picked - lse, 0.0)
    value_ent = jnp.where(live, lse - moment / mass, 0.0)
    share = rows // groups
    rank = (dest // rows) * share + dest % share
    hit = lax.broadcasted_iota(jnp.int32, (rows, rows), 0) == rank[None, :]
    sent = [jnp.sum(jnp.where(hit, v[None, :], 0.0), axis=1).reshape(groups, share) for v in (value_lp, value_ent)]
    got = lax.all_to_all(jnp.concatenate(sent, axis=1), ("z", "y", "core"), 0, 0, tiled=True)
    return got[:, :share].reshape(rows), got[:, share:].reshape(rows)


def solution(mesh):
    tensor = mesh.devices.shape[1]
    fine = Mesh(mesh.devices.reshape(RING, RING, 2, tensor), ("z", "y", "core", "tensor"))
    group = ("z", "y", "core")
    in_specs = (P(group, "tensor"), P(), P(None, ("tensor", "z", "y", "core")), P(group), P(group), P(group))
    return jax.shard_map(body, mesh=fine, in_specs=in_specs, out_specs=(P(group), P(group)), check_vma=False)
```

time: 173 us -> 104 us (0.60)
  waiting for transfers between devices: 79 us -> 0 us
  Pallas kernels: 0 us -> 75.1 us
  starting transfers between devices: 21.4 us -> 0 us
  between operations: 14.9 us -> 1.37 us
  blocking collectives: 33.6 us -> 21.1 us
  matrix products: 10.5 us -> 0 us
  other arithmetic: 8.21 us -> 0.6 us
    pallas_call x0 -> x1, Pallas kernels: none -> 75.1 us  [head(): pl.pallas_call(head_kernel, out_shape=jax.ShapeDtypeStruct((2 * TENSORS,...]
    all_gather x1 -> x0, waiting for transfers between devices: 69.9 us -> none  [body(): piece = lax.all_gather(spread, 'zy', axis=0, tiled=True)]
    ppermute x6 -> x0, starting transfers between devices: 21.4 us -> none  [the longest x3 10.1 us: body(): lax.ppermute(hidden, 'tensor', [((i + step) % tensors, i) for i in range(...]
    dot_general x1 -> x0, matrix products: 10.5 us -> none  [body(): lax.dot_general(piece, normed, (((1,), (1,)), ((), ())), preferred_elemen...]
    all_gather x1 -> x0, blocking collectives: 9.34 us -> none  [body(): top, mass, moment, picked = merge(lax.all_gather(pair, 'tensor', axis=0))]
    ppermute x6 -> x0, waiting for transfers between devices: 9.08 us -> none  [the longest x3 8.43 us: body(): lax.ppermute(hidden, 'tensor', [((i + step) % tensors, i) for i in range(...]
    reduce_sum x4 -> x1, other arithmetic: 5.39 us -> 0.03 us  [body(): mass = jnp.sum(parts[:, 1] * factor, axis=0)]
    all_to_all x1, blocking collectives: 24.2 us -> 21.1 us  [body(): lax.all_to_all(jnp.concatenate(sent, axis=1), ('z', 'y', 'core'), 0, 0, t...]
  transfers between devices with their start and end apart: 7 -> 0, of which waited for: 5 -> 0; matrix products, arithmetic and copies ran while one was open for 3% -> 0% of each run, Pallas kernels for 0% -> 0%
where the time goes in v2:
time: 104 us
  Pallas kernels  75.1 us (72%)
  blocking collectives  21.1 us (20%)
  local copies, waits for them, and re-layouts  5.6 us (5%)
  between operations  1.37 us (1%)
    pallas_call x1, Pallas kernels, head(): pl.pallas_call(head_kernel, out_shape=jax.ShapeDtypeStruct((2 * TENSORS,...  75.1 us
    all_to_all x1, blocking collectives, body(): lax.all_to_all(jnp.concatenate(sent, axis=1), ('z', 'y', 'core'), 0, 0, t...  21.1 us

profile of v2, /device:TPU:1, one launch (start us, length us, event | category | flops | bytes accessed | tf_op | source)
XLA Modules:
  0.0 103.7 jit_solution(14724784079910698652)
XLA Ops:
  0.6 0.9 slice.33.main_hbm
  1.5 0.7 slice.34
  2.3 0.0 copy-start.1
  2.3 0.7 copy-done.1
  2.9 0.0 copy-start
  2.9 0.2 copy.23.gain_ref
  3.2 0.7 copy-done
  3.9 0.0 copy-start.2
  3.9 0.1 copy.22
  4.0 0.5 copy-done.2
  4.6 75.1 %shard_map.77 = f32[8,8,512]{2,1,0:T(8,128)S(1)} custom-call(bf16[48,1024]{1,0:T(8,128)(2,1)S(1)} %slice.33.main_hbm, bf16[16,128]{1,0:T(8,128)(2,1)S(1)} %reshape.54.rest_hbm, bf16[256,512]{1,0:T(8,128)(2,1)S(1)} %bitcast.30, s32[1,512]{1,0:T(1,128)S(1)} %bitcast.31, f32[1024,1]{1,0:T(8,128)S(1)} %copy.23.gain_ref), custom_call_target="tpu_custom_call" | custom-call | tf_op jit(solution)/shard_map/pallas_call | solution.py:293
  79.7 0.0 copy-start.3
  79.7 0.1 fusion.16
  80.4 0.0 copy-done.3
  80.5 0.4 select_reduce_fusion.1
  80.9 0.1 reshape.57
  81.0 0.1 reshape.58
  81.1 0.1 pad_maximum_fusion
  81.2 21.1 %all_to_all.12 = f32[128,1,8]{2,1,0:T(1,128)S(1)} all-to-all(f32[128,1,8]{2,1,0:T(1,128)S(1)} %bitcast.33), channel_id=1, replica_groups=mesh['z'=8,'y'=8,'core'=2,'tensor'=4] {'z','y','core'}, dimensions={0} | all-to-all | bytes 8192 | tf_op jit(solution)/shard_map/all_to_all | solution.py:344
  102.3 0.1 fusion.17
  102.4 0.7 reshape.59
  103.1 0.7 reshape.60
  (5 shorter events, 0.1 us)
Async XLA Ops:
  2.3 0.7 copy-start.1
  2.9 0.9 copy-start
  3.9 0.7 copy-start.2
  79.7 0.7 copy-start.3

commit v3 on v2

--- a/solution.py
+++ b/solution.py
@@ -18,9 +18,11 @@
     return ((i + 1) >> 1) * (1 - 2 * (i & 1))
 
 
-def head_kernel(main_hbm, rest_hbm, hid_hbm, code_hbm, gain_ref, out_ref,
+def head_kernel(main_hbm, rest_hbm, hid_hbm, code_hbm, gain_ref, place_ref, live_ref, out_ref,
                 wbuf, lbuf, hbuf, cbuf, normed, wide_rest, rest, stats, packed, gath,
-                w_recv, w_send, h_recv, h_send, c_sem, s_recv, s_send, local_sem):
+                select, values, line_out, line_in, plane_out, plane_in,
+                w_recv, w_send, h_recv, h_send, c_sem, s_recv, s_send, local_sem,
+                l_recv, l_send, p_recv, p_send):
     z, y = lax.axis_index("z"), lax.axis_index("y")
     core, x = lax.axis_index("core"), lax.axis_index("tensor")
     rows = hid_hbm.shape[1]
@@ -43,7 +45,7 @@
     slot0 = q * RING + p
 
     locals_ = [
-        pltpu.make_async_copy(main_hbm, wbuf.at[slot0], local_sem.at[0]),
+        pltpu.make_async_copy(main_hbm.at[pl.ds(0, MAIN)], wbuf.at[slot0], local_sem.at[0]),
         pltpu.make_async_copy(rest_hbm, lbuf.at[slot0], local_sem.at[1]),
         pltpu.make_async_copy(hid_hbm, hbuf.at[core, x], local_sem.at[2]),
         pltpu.make_async_copy(code_hbm, cbuf.at[core], local_sem.at[3]),
@@ -141,6 +143,10 @@
     states(core, x + 2, 0, partner).wait_recv()
     states(core, x + 2, 3, partner).start()
     both(1, 4, 8)
+
+    spots = lax.broadcasted_iota(jnp.int32, select.shape, 1)
+    select[...] = jnp.where(spots == place_ref[...], 1.0, 0.0).astype(jnp.bfloat16)
+    line_out[...] = jnp.zeros(line_out.shape, F32)
 
     for d in range(TENSORS):
         states(1 - core, x + d, 0, partner).wait_recv()
@@ -254,6 +260,66 @@
     own = pltpu.make_async_copy(packed.at[core], gath.at[who], local_sem.at[0])
     own.start()
 
+    own.wait()
+    for n, peer in enumerate(peers):
+        result_from(n, peer).wait_recv()
+
+    tops = gath[:, 0, :]
+    top = jnp.max(tops, axis=0, keepdims=True)
+    factor = jnp.exp(tops - top)
+    mass = jnp.sum(gath[:, 1, :] * factor, axis=0, keepdims=True)
+    moment = jnp.sum(gath[:, 2, :] * factor, axis=0, keepdims=True)
+    picked = jnp.sum(gath[:, 3, :], axis=0, keepdims=True)
+    live = live_ref[...] > 0
+    lse = top + jnp.log(mass)
+    values[pl.ds(0, 1), :] = jnp.where(live, picked - lse, 0.0)
+    values[pl.ds(1, 1), :] = jnp.where(live, lse - moment / mass, 0.0)
+    exact = values[...]
+    high = exact.astype(jnp.bfloat16)
+    left = exact - high.astype(F32)
+    middle = left.astype(jnp.bfloat16)
+    low = (left - middle.astype(F32)).astype(jnp.bfloat16)
+    ordered = jnp.zeros((2, select.shape[1]), F32)
+    for term in (low, middle, high):
+        ordered += jnp.dot(term, select[...], preferred_element_type=F32)
+    for n in range(RING):
+        line_out[n, pl.ds(0, 2), :] = ordered[:, n * 128:(n + 1) * 128]
+
+    def along_line(d, other, source):
+        return pltpu.make_async_remote_copy(
+            src_ref=line_out.at[other], dst_ref=line_in.at[source],
+            send_sem=l_send.at[d], recv_sem=l_recv.at[source],
+            device_id=(other, y, core, x), device_id_type=pl.DeviceIdType.MESH)
+
+    own_line = pltpu.make_async_copy(line_out.at[z], line_in.at[z], local_sem.at[1])
+    for d in range(1, RING):
+        along_line(d, wrap(z + d), z).start()
+    own_line.start()
+    own_line.wait()
+    for d in range(1, RING):
+        along_line(d, wrap(z + d), wrap(z + d)).wait_recv()
+    first_half, second_half = line_in[:, 0, :], line_in[:, 1, :]
+    lanes = lax.broadcasted_iota(jnp.int32, (RING, 128), 1)
+    for n in range(2 * RING):
+        plane_out[n] = jnp.where(
+            lanes < 4, pltpu.roll(first_half, (128 - 4 * n) % 128, 1),
+            pltpu.roll(second_half, (132 - 4 * n) % 128, 1))
+    here = y * 2 + core
+
+    def across_plane(d, other, source):
+        return pltpu.make_async_remote_copy(
+            src_ref=plane_out.at[other], dst_ref=plane_in.at[source],
+            send_sem=p_send.at[d], recv_sem=p_recv.at[source],
+            device_id=(z, other >> 1, other & 1, x), device_id_type=pl.DeviceIdType.MESH)
+
+    def turn(d):
+        return (here + d) & (2 * RING - 1)
+
+    own_plane = pltpu.make_async_copy(plane_out.at[here], plane_in.at[here], local_sem.at[2])
+    for d in range(1, 2 * RING):
+        across_plane(d, turn(d), here).start()
+    own_plane.start()
+
     for t in range(4):
         sent(q * RING + wrap(p - t), 0)
     for t in range(3):
@@ -277,14 +343,18 @@
     for d in range(TENSORS):
         states(core, x + d, 3, partner).wait_send()
     codes.wait_send()
-    own.wait()
     for n, peer in enumerate(peers):
-        result_from(n, peer).wait_recv()
         result(n, peer).wait_send()
-    out_ref[...] = gath[...]
-
-
-def head(main, rest, hid, code, gain):
+    for d in range(1, RING):
+        along_line(d, wrap(z + d), z).wait_send()
+    own_plane.wait()
+    for d in range(1, 2 * RING):
+        across_plane(d, turn(d), here).wait_send()
+        across_plane(d, turn(d), turn(d)).wait_recv()
+    out_ref[...] = plane_in[...]
+
+
+def head(main, rest, hid, code, gain, place, live):
     rows, feats, slots = hid.shape[1], hid.shape[0], RING * RING
     depth = TENSORS * feats
     any_space = pl.BlockSpec(memory_space=pl.ANY)
@@ -292,8 +362,8 @@
     dma = pltpu.SemaphoreType.DMA
     return pl.pallas_call(
         head_kernel,
-        out_shape=jax.ShapeDtypeStruct((2 * TENSORS, 8, rows), F32),
-        in_specs=[any_space] * 4 + [vmem],
+        out_shape=jax.ShapeDtypeStruct((2 * RING, RING, 128), F32),
+        in_specs=[any_space] * 4 + [vmem] * 3,
         out_specs=vmem,
         scratch_shapes=[
             pltpu.VMEM((slots, MAIN, depth), jnp.bfloat16),
@@ -306,12 +376,19 @@
             pltpu.VMEM((4, 8, 2 * rows), F32),
             pltpu.VMEM((2, 8, rows), F32),
             pltpu.VMEM((2 * TENSORS, 8, rows), F32),
+            pltpu.VMEM((rows, RING * 128), jnp.bfloat16),
+            pltpu.VMEM((2, rows), F32),
+            pltpu.VMEM((RING, 8, 128), F32),
+            pltpu.VMEM((RING, 8, 128), F32),
+            pltpu.VMEM((2 * RING, RING, 128), F32),
+            pltpu.VMEM((2 * RING, RING, 128), F32),
             dma((2, slots)), dma((4, 2, slots)), dma((2, TENSORS)), dma((4, TENSORS)),
             dma((2,)), dma((2 * TENSORS,)), dma((2 * TENSORS,)), dma((4,)),
+            dma((RING,)), dma((RING,)), dma((2 * RING,)), dma((2 * RING,)),
         ],
         compiler_params=pltpu.CompilerParams(
             collective_id=0, has_side_effects=True, vmem_limit_bytes=48 << 20),
-    )(main, rest, hid, code, gain)
+    )(main, rest, hid, code, gain, place, live)
 
 
 def body(hidden, gain, head_weight, targets, row_count, dest):
@@ -327,22 +404,14 @@
     slot = jnp.where(near == 0, yi * RING + zi, zi * RING + yi)
     index = jnp.where(column < MAIN, slot * MAIN + column, RING * RING * MAIN + slot * 2 + column - MAIN)
     code = ((owner * 2 + near) * 4096 + index).reshape(1, rows)
-    parts = head(turned[:MAIN], rest, hidden.T, code, gain.reshape(-1, 1))
-    top = jnp.max(parts[:, 0], axis=0)
-    factor = jnp.exp(parts[:, 0] - top[None])
-    mass = jnp.sum(parts[:, 1] * factor, axis=0)
-    moment = jnp.sum(parts[:, 2] * factor, axis=0)
-    picked = jnp.sum(parts[:, 3], axis=0)
-    live = jnp.arange(rows, dtype=jnp.int32) < row_count[0]
-    lse = top + jnp.log(mass)
-    value_lp = jnp.where(live, picked - lse, 0.0)
-    value_ent = jnp.where(live, lse - moment / mass, 0.0)
     share = rows // groups
     rank = (dest // rows) * share + dest % share
-    hit = lax.broadcasted_iota(jnp.int32, (rows, rows), 0) == rank[None, :]
-    sent = [jnp.sum(jnp.where(hit, v[None, :], 0.0), axis=1).reshape(groups, share) for v in (value_lp, value_ent)]
-    got = lax.all_to_all(jnp.concatenate(sent, axis=1), ("z", "y", "core"), 0, 0, tiled=True)
-    return got[:, :share].reshape(rows), got[:, share:].reshape(rows)
+    line = rows // RING
+    place = (rank // line) * 128 + rank % line
+    live = (jnp.arange(rows, dtype=jnp.int32) < row_count[0]).astype(jnp.int32)
+    got = head(turned, rest, hidden.T, code, gain.reshape(-1, 1), place.reshape(-1, 1), live.reshape(1, -1))
+    got = jnp.moveaxis(got[:, :, :2 * share], 1, 0)
+    return got[:, :, :share].reshape(rows), got[:, :, share:].reshape(rows)
 
 
 def solution(mesh):

time: 104 us -> 94.2 us (0.906)
  blocking collectives: 21.1 us -> 0 us
  Pallas kernels: 75.1 us -> 87.2 us
  local copies, waits for them, and re-layouts: 5.6 us -> 3.94 us
    all_to_all x1 -> x0, blocking collectives: 21.1 us -> none  [body(): lax.all_to_all(jnp.concatenate(sent, axis=1), ('z', 'y', 'core'), 0, 0, t...]
    pallas_call x1, Pallas kernels: 75.1 us -> 87.2 us  [head(): pl.pallas_call(head_kernel, out_shape=jax.ShapeDtypeStruct((2 * RING, RIN...]
where the time goes in v3:
time: 94.2 us; the launch traced here: 93.9 us
  Pallas kernels  87.2 us (93%)
  local copies, waits for them, and re-layouts  3.94 us (4%)
  other arithmetic  1.44 us (2%)
  between operations  1.4 us (1%)
    pallas_call x1, Pallas kernels, head(): pl.pallas_call(head_kernel, out_shape=jax.ShapeDtypeStruct((2 * RING, RIN...  87.2 us

profile of v3, /device:TPU:1, one launch (start us, length us, event | category | flops | bytes accessed | tf_op | source)
XLA Modules:
  0.0 93.9 jit_solution(14471579910992265160)
XLA Ops:
  0.6 0.0 copy-start.1
  1.3 0.7 select_add_fusion
  2.1 0.7 fusion.5
  2.8 0.7 slice.16
  3.5 0.1 copy.11.place_ref
  3.7 0.0 copy-done.1
  3.7 0.0 copy-start.2
  3.7 0.1 copy.9
  3.8 0.5 copy-done.2
  4.4 0.0 copy-start
  4.4 0.2 copy.10.gain_ref
  4.6 0.7 copy-done
  5.3 87.2 %shard_map.77 = f32[16,8,128]{2,1,0:T(8,128)S(1)} custom-call(bf16[50,1024]{1,0:T(8,128)(2,1)S(1)} %bitcast.11, bf16[16,128]{1,0:T(8,128)(2,1)S(1)} %reshape.33.rest_hbm, bf16[256,512]{1,0:T(8,128)(2,1)S(1)} %bitcast.9, s32[1,512]{1,0:T(1,128)S(1)} %bitcast.12, f32[1024,1]{1,0:T(8,128)S(1)} %copy.10.gain_ref, s32[512,1]{1,0:T(8,128)S(1)} %copy.11.place_ref, ...), custom_call_target="tpu_custom_call" | custom-call | tf_op jit(solution)/shard_map/pallas_call | solution.py:363
  92.4 0.1 fusion.15
  92.5 0.7 reshape.38
  93.2 0.7 reshape.37
  (5 shorter events, 0.1 us)
Async XLA Ops:
  0.6 3.0 %copy-start.1 = (bf16[512,256]{1,0:T(8,128)(2,1)S(1)}, bf16[512,256]{1,0:T(8,128)(2,1)}, u32[]{:S(2)}) copy-start(bf16[512,256]{1,0:T(8,128)(2,1)} %param.6) | copy-start | bytes 786436
  3.7 0.7 copy-start.2
  4.4 0.9 copy-start

commit v4 on v3

--- a/solution.py
+++ b/solution.py
@@ -21,7 +21,7 @@
 def head_kernel(main_hbm, rest_hbm, hid_hbm, code_hbm, gain_ref, place_ref, live_ref, out_ref,
                 wbuf, lbuf, hbuf, cbuf, normed, wide_rest, rest, stats, packed, gath,
                 select, values, line_out, line_in, plane_out, plane_in,
-                w_recv, w_send, h_recv, h_send, c_sem, s_recv, s_send, local_sem,
+                b_recv, b_send, m_recv, m_send, r_recv, r_send, h_recv, h_send, c_sem, s_recv, s_send, local_sem,
                 l_recv, l_send, p_recv, p_send):
     z, y = lax.axis_index("z"), lax.axis_index("y")
     core, x = lax.axis_index("core"), lax.axis_index("tensor")
@@ -42,7 +42,7 @@
     right1, left1 = at(wrap(p + 1), q), at(wrap(p - 1), q)
     right2, left2 = at(p, wrap(q + 1)), at(p, wrap(q - 1))
     partner = at_x(x, 1 - core)
-    slot0 = q * RING + p
+    slot0 = q * RING
 
     locals_ = [
         pltpu.make_async_copy(main_hbm.at[pl.ds(0, MAIN)], wbuf.at[slot0], local_sem.at[0]),
@@ -60,26 +60,28 @@
         copy.wait()
     pl.semaphore_wait(barrier, 4 + len(peers))
 
-    def block(slot, kind, target):
+    def block(index, landing, kind, target):
         return [
             pltpu.make_async_remote_copy(
-                src_ref=buf.at[slot], dst_ref=buf.at[slot],
-                send_sem=w_send.at[kind, n, slot], recv_sem=w_recv.at[n, slot],
+                src_ref=buf.at[slot0 + index], dst_ref=buf.at[slot0 + landing],
+                send_sem=b_send.at[kind, n, index], recv_sem=b_recv.at[n, landing],
                 device_id=target, device_id_type=pl.DeviceIdType.MESH)
             for n, buf in enumerate((wbuf, lbuf))
         ]
 
-    def start(slot, kind, target):
-        for copy in block(slot, kind, target):
-            copy.start()
-
-    def arrive(slot):
-        for copy in block(slot, 0, right1):
-            copy.wait_recv()
-
-    def sent(slot, kind):
-        for copy in block(slot, kind, right1):
-            copy.wait_send()
+    def message(group, half, kind, target):
+        part = wbuf.at[pl.ds(group * RING + half * 4, 4)]
+        return pltpu.make_async_remote_copy(
+            src_ref=part, dst_ref=part,
+            send_sem=m_send.at[kind, group, half], recv_sem=m_recv.at[group, half],
+            device_id=target, device_id_type=pl.DeviceIdType.MESH)
+
+    def remainder(group, kind, target):
+        part = lbuf.at[pl.ds(group * RING, RING)]
+        return pltpu.make_async_remote_copy(
+            src_ref=part, dst_ref=part,
+            send_sem=r_send.at[kind, group], recv_sem=r_recv.at[group],
+            device_id=target, device_id_type=pl.DeviceIdType.MESH)
 
     def states(cc, xx, kind, target):
         xs = (xx + 2 * TENSORS) & (TENSORS - 1)
@@ -92,27 +94,28 @@
         src_ref=cbuf.at[core], dst_ref=cbuf.at[core], send_sem=c_sem.at[0], recv_sem=c_sem.at[1],
         device_id=partner, device_id_type=pl.DeviceIdType.MESH)
     way = 1 - 2 * core
-    start(slot0, 0, right1)
-    start(slot0, 1, left1)
+    for copy in block(0, 1, 0, right1) + block(0, 2, 1, left1):
+        copy.start()
     states(core, x, 0, at_x(x + 1, core)).start()
     states(core, x, 1, at_x(x - 1, core)).start()
     states(core, x, 3, partner).start()
     codes.start()
-    start(slot0, 2, right2)
-    start(slot0, 3, left2)
 
     def first(i):
-        slot = q * RING + wrap(p + zigzag(i))
-        arrive(slot)
+        for copy in block(i, i, 0, right1):
+            copy.wait_recv()
+        onward = []
         if i in (1, 3, 5):
-            start(slot, 0, right1)
+            onward = block(i, i + 2, 0, right1)
         if i in (2, 4):
-            start(slot, 1, left1)
-        start(slot, 2, right2)
-        start(slot, 3, left2)
+            onward = block(i, i + 2, 1, left1)
+        for copy in onward:
+            copy.start()
 
     for i in range(1, 4):
         first(i)
+    message(q, 0, 0, right2).start()
+    message(q, 0, 1, left2).start()
     for d in (-1, 1):
         states(core, x + d, 0, partner).wait_recv()
     states(core, x - way, 2, at_x(x + way, core)).start()
@@ -121,32 +124,35 @@
     for i in range(4, 8):
         first(i)
 
-    def from_left(t, i, forward):
-        slot = wrap(q - t) * RING + wrap(p + zigzag(i))
-        arrive(slot)
-        if forward:
-            start(slot, 2, right2)
-
-    def from_right(t, i, forward):
-        slot = wrap(q + t) * RING + wrap(p + zigzag(i))
-        arrive(slot)
-        if forward:
-            start(slot, 3, left2)
-
-    def both(t, low, high):
-        @pl.loop(low, high)
-        def _(i):
-            from_left(t, i, True)
-            from_right(t, i, True)
-
-    both(1, 0, 4)
-    states(core, x + 2, 0, partner).wait_recv()
-    states(core, x + 2, 3, partner).start()
-    both(1, 4, 8)
+    remainder(q, 0, right2).start()
+    remainder(q, 1, left2).start()
+    message(q, 1, 0, right2).start()
+    message(q, 1, 1, left2).start()
+
+    def second(t, half):
+        back, ahead = wrap(q - t), wrap(q + t)
+        if half == 1:
+            remainder(back, 0, right2).wait_recv()
+            if t < 4:
+                remainder(back, 0, right2).start()
+                remainder(ahead, 1, left2).wait_recv()
+            if t < 3:
+                remainder(ahead, 1, left2).start()
+        if t < 4 or half == 0:
+            message(back, half, 0, right2).wait_recv()
+        if t < 3 or (t == 3 and half == 0):
+            message(back, half, 0, right2).start()
+        if t < 4 or half == 1:
+            message(ahead, half, 1, left2).wait_recv()
+        if t < 3 or (t == 3 and half == 1):
+            message(ahead, half, 1, left2).start()
 
     spots = lax.broadcasted_iota(jnp.int32, select.shape, 1)
     select[...] = jnp.where(spots == place_ref[...], 1.0, 0.0).astype(jnp.bfloat16)
     line_out[...] = jnp.zeros(line_out.shape, F32)
+    states(core, x + 2, 0, partner).wait_recv()
+    states(core, x + 2, 3, partner).start()
+    second(1, 0)
 
     for d in range(TENSORS):
         states(1 - core, x + d, 0, partner).wait_recv()
@@ -194,34 +200,24 @@
         weights = wbuf[pl.ds(pl.multiple_of(g * RING, RING), RING)].reshape(RING * MAIN, -1)
         update(weights, RING * MAIN, g * (RING * MAIN), r)
 
-    @pl.loop(0, 8)
-    def _(i):
-        from_left(2, i, True)
-        from_right(2, i, True)
-        unit(i)
-
-    @pl.loop(0, 4)
-    def _(i):
-        from_left(3, i, True)
-        from_right(3, i, False)
-        unit(8 + i)
-
-    @pl.loop(4, 8)
-    def _(i):
-        from_left(3, i, False)
-        from_right(3, i, True)
-        unit(8 + i)
-
-    @pl.loop(0, 4)
-    def _(i):
-        from_left(4, i, False)
-        unit(16 + 2 * i)
-        from_right(4, i + 4, False)
-        unit(17 + 2 * i)
-
-    @pl.loop(24, 32)
-    def _(u):
-        unit(u)
+    def units(low, high):
+        @pl.loop(low, high)
+        def _(u):
+            unit(u)
+
+    second(1, 1)
+    units(0, 4)
+    second(2, 0)
+    units(4, 8)
+    second(2, 1)
+    units(8, 12)
+    second(3, 0)
+    units(12, 16)
+    second(3, 1)
+    units(16, 28)
+    second(4, 0)
+    second(4, 1)
+    units(28, 32)
 
     total = RING * RING * 2
     wide_rest[...] = lbuf[...].astype(F32).reshape(total * 8, 128)
@@ -320,22 +316,21 @@
         across_plane(d, turn(d), here).start()
     own_plane.start()
 
+    for i in (0, 1, 3, 5):
+        for copy in block(i, i, 0, right1):
+            copy.wait_send()
+    for i in (0, 2, 4):
+        for copy in block(i, i, 1, left1):
+            copy.wait_send()
     for t in range(4):
-        sent(q * RING + wrap(p - t), 0)
-    for t in range(3):
-        sent(q * RING + wrap(p + t), 1)
-
-    @pl.loop(0, 8)
-    def _(i):
-        pp = wrap(p + zigzag(i))
-        for t in range(3):
-            sent(wrap(q - t) * RING + pp, 2)
-            sent(wrap(q + t) * RING + pp, 3)
-
-    @pl.loop(0, 4)
-    def _(i):
-        sent(wrap(q - 3) * RING + wrap(p + zigzag(i)), 2)
-        sent(wrap(q + 3) * RING + wrap(p + zigzag(i + 4)), 3)
+        back, ahead = wrap(q - t), wrap(q + t)
+        remainder(back, 0, right2).wait_send()
+        message(back, 0, 0, right2).wait_send()
+        message(ahead, 1, 1, left2).wait_send()
+        if t < 3:
+            remainder(ahead, 1, left2).wait_send()
+            message(back, 1, 0, right2).wait_send()
+            message(ahead, 0, 1, left2).wait_send()
 
     states(core, x, 0, partner).wait_send()
     states(core, x, 1, partner).wait_send()
@@ -382,7 +377,8 @@
             pltpu.VMEM((RING, 8, 128), F32),
             pltpu.VMEM((2 * RING, RING, 128), F32),
             pltpu.VMEM((2 * RING, RING, 128), F32),
-            dma((2, slots)), dma((4, 2, slots)), dma((2, TENSORS)), dma((4, TENSORS)),
+            dma((2, RING)), dma((2, 2, RING)), dma((RING, 2)), dma((2, RING, 2)), dma((RING,)), dma((2, RING)),
+            dma((2, TENSORS)), dma((4, TENSORS)),
             dma((2,)), dma((2 * TENSORS,)), dma((2 * TENSORS,)), dma((4,)),
             dma((RING,)), dma((RING,)), dma((2 * RING,)), dma((2 * RING,)),
         ],
@@ -401,7 +397,10 @@
     device = (targets // cols) % groups
     near, zy = device % 2, device // 2
     zi, yi = zy // RING, zy % RING
-    slot = jnp.where(near == 0, yi * RING + zi, zi * RING + yi)
+    z, y = lax.axis_index("z"), lax.axis_index("y")
+    gone = (jnp.where(near == 0, zi - z, yi - y) + RING) % RING
+    order = jnp.where(gone < RING // 2, 2 * gone, 2 * (RING - gone) - 1)
+    slot = jnp.where(near == 0, yi, zi) * RING + order
     index = jnp.where(column < MAIN, slot * MAIN + column, RING * RING * MAIN + slot * 2 + column - MAIN)
     code = ((owner * 2 + near) * 4096 + index).reshape(1, rows)
     share = rows // groups

time: 94.2 us -> 90.9 us (0.965)
  Pallas kernels: 87.2 us -> 83.8 us
    pallas_call x1, Pallas kernels: 87.2 us -> 83.8 us  [head(): pl.pallas_call(head_kernel, out_shape=jax.ShapeDtypeStruct((2 * RING, RIN...]
where the time goes in v4:
time: 90.9 us; the launch traced here: 90.6 us
  Pallas kernels  83.8 us (92%)
  local copies, waits for them, and re-layouts  3.94 us (4%)
  other arithmetic  1.45 us (2%)
  between operations  1.41 us (2%)
    pallas_call x1, Pallas kernels, head(): pl.pallas_call(head_kernel, out_shape=jax.ShapeDtypeStruct((2 * RING, RIN...  83.8 us

profile of v4, /device:TPU:1, one launch (start us, length us, event | category | flops | bytes accessed | tf_op | source)
XLA Modules:
  0.0 90.6 jit_solution(3330553668257823416)
XLA Ops:
  0.6 0.0 copy-start.1
  1.3 0.7 select_add_fusion
  2.1 0.7 fusion.6
  2.8 0.7 slice.16
  3.5 0.1 copy.11.place_ref
  3.7 0.0 copy-done.1
  3.7 0.0 copy-start.2
  3.7 0.1 copy.9
  3.8 0.5 copy-done.2
  4.4 0.0 copy-start
  4.4 0.2 copy.10.gain_ref
  4.6 0.7 copy-done
  5.3 83.8 %shard_map.77 = f32[16,8,128]{2,1,0:T(8,128)S(1)} custom-call(bf16[50,1024]{1,0:T(8,128)(2,1)S(1)} %bitcast.11, bf16[16,128]{1,0:T(8,128)(2,1)S(1)} %reshape.33.rest_hbm, bf16[256,512]{1,0:T(8,128)(2,1)S(1)} %bitcast.9, s32[1,512]{1,0:T(1,128)S(1)} %bitcast.12, f32[1024,1]{1,0:T(8,128)S(1)} %copy.10.gain_ref, s32[512,1]{1,0:T(8,128)S(1)} %copy.11.place_ref, ...), custom_call_target="tpu_custom_call" | custom-call | tf_op jit(solution)/shard_map/pallas_call | solution.py:358
  89.1 0.1 fusion.16
  89.2 0.7 reshape.38
  89.9 0.7 reshape.37
  (5 shorter events, 0.1 us)
Async XLA Ops:
  0.6 3.0 %copy-start.1 = (bf16[512,256]{1,0:T(8,128)(2,1)S(1)}, bf16[512,256]{1,0:T(8,128)(2,1)}, u32[]{:S(2)}) copy-start(bf16[512,256]{1,0:T(8,128)(2,1)} %param.6) | copy-start | bytes 786436
  3.7 0.7 copy-start.2
  4.4 0.9 copy-start

commit v5 on v4

--- a/solution.py
+++ b/solution.py
@@ -21,7 +21,7 @@
 def head_kernel(main_hbm, rest_hbm, hid_hbm, code_hbm, gain_ref, place_ref, live_ref, out_ref,
                 wbuf, lbuf, hbuf, cbuf, normed, wide_rest, rest, stats, packed, gath,
                 select, values, line_out, line_in, plane_out, plane_in,
-                b_recv, b_send, m_recv, m_send, r_recv, r_send, h_recv, h_send, c_sem, s_recv, s_send, local_sem,
+                b_recv, b_send, m_recv, m_send, o_recv, o_send, r_recv, r_send, h_recv, h_send, c_sem, s_recv, s_send, local_sem,
                 l_recv, l_send, p_recv, p_send):
     z, y = lax.axis_index("z"), lax.axis_index("y")
     core, x = lax.axis_index("core"), lax.axis_index("tensor")
@@ -76,6 +76,13 @@
             send_sem=m_send.at[kind, group, half], recv_sem=m_recv.at[group, half],
             device_id=target, device_id_type=pl.DeviceIdType.MESH)
 
+    def single(group, index, kind, target):
+        part = wbuf.at[group * RING + index]
+        return pltpu.make_async_remote_copy(
+            src_ref=part, dst_ref=part,
+            send_sem=o_send.at[kind, index], recv_sem=o_recv.at[kind, index],
+            device_id=target, device_id_type=pl.DeviceIdType.MESH)
+
     def remainder(group, kind, target):
         part = lbuf.at[pl.ds(group * RING, RING)]
         return pltpu.make_async_remote_copy(
@@ -96,6 +103,8 @@
     way = 1 - 2 * core
     for copy in block(0, 1, 0, right1) + block(0, 2, 1, left1):
         copy.start()
+    single(q, 0, 0, right2).start()
+    single(q, 0, 1, left2).start()
     states(core, x, 0, at_x(x + 1, core)).start()
     states(core, x, 1, at_x(x - 1, core)).start()
     states(core, x, 3, partner).start()
@@ -111,11 +120,11 @@
             onward = block(i, i + 2, 1, left1)
         for copy in onward:
             copy.start()
+        single(q, i, 0, right2).start()
+        single(q, i, 1, left2).start()
 
     for i in range(1, 4):
         first(i)
-    message(q, 0, 0, right2).start()
-    message(q, 0, 1, left2).start()
     for d in (-1, 1):
         states(core, x + d, 0, partner).wait_recv()
     states(core, x - way, 2, at_x(x + way, core)).start()
@@ -126,8 +135,6 @@
 
     remainder(q, 0, right2).start()
     remainder(q, 1, left2).start()
-    message(q, 1, 0, right2).start()
-    message(q, 1, 1, left2).start()
 
     def second(t, half):
         back, ahead = wrap(q - t), wrap(q + t)
@@ -138,21 +145,28 @@
                 remainder(ahead, 1, left2).wait_recv()
             if t < 3:
                 remainder(ahead, 1, left2).start()
-        if t < 4 or half == 0:
+        if t == 1:
+            for index in range(4 * half, 4 * half + 4):
+                single(back, index, 0, right2).wait_recv()
+        elif t < 4 or half == 0:
             message(back, half, 0, right2).wait_recv()
         if t < 3 or (t == 3 and half == 0):
             message(back, half, 0, right2).start()
-        if t < 4 or half == 1:
+        if t == 1:
+            for index in range(4 * half, 4 * half + 4):
+                single(ahead, index, 1, left2).wait_recv()
+        elif t < 4 or half == 1:
             message(ahead, half, 1, left2).wait_recv()
         if t < 3 or (t == 3 and half == 1):
             message(ahead, half, 1, left2).start()
 
+    states(core, x + 2, 0, partner).wait_recv()
+    states(core, x + 2, 3, partner).start()
+    second(1, 0)
     spots = lax.broadcasted_iota(jnp.int32, select.shape, 1)
     select[...] = jnp.where(spots == place_ref[...], 1.0, 0.0).astype(jnp.bfloat16)
     line_out[...] = jnp.zeros(line_out.shape, F32)
-    states(core, x + 2, 0, partner).wait_recv()
-    states(core, x + 2, 3, partner).start()
-    second(1, 0)
+    second(1, 1)
 
     for d in range(TENSORS):
         states(1 - core, x + d, 0, partner).wait_recv()
@@ -205,9 +219,8 @@
         def _(u):
             unit(u)
 
-    second(1, 1)
+    second(2, 0)
     units(0, 4)
-    second(2, 0)
     units(4, 8)
     second(2, 1)
     units(8, 12)
@@ -322,13 +335,18 @@
     for i in (0, 2, 4):
         for copy in block(i, i, 1, left1):
             copy.wait_send()
+    for index in range(RING):
+        single(q, index, 0, right2).wait_send()
+        single(q, index, 1, left2).wait_send()
     for t in range(4):
         back, ahead = wrap(q - t), wrap(q + t)
         remainder(back, 0, right2).wait_send()
-        message(back, 0, 0, right2).wait_send()
-        message(ahead, 1, 1, left2).wait_send()
+        if t > 0:
+            message(back, 0, 0, right2).wait_send()
+            message(ahead, 1, 1, left2).wait_send()
         if t < 3:
             remainder(ahead, 1, left2).wait_send()
+        if 0 < t < 3:
             message(back, 1, 0, right2).wait_send()
             message(ahead, 0, 1, left2).wait_send()
 
@@ -377,7 +395,8 @@
             pltpu.VMEM((RING, 8, 128), F32),
             pltpu.VMEM((2 * RING, RING, 128), F32),
             pltpu.VMEM((2 * RING, RING, 128), F32),
-            dma((2, RING)), dma((2, 2, RING)), dma((RING, 2)), dma((2, RING, 2)), dma((RING,)), dma((2, RING)),
+            dma((2, RING)), dma((2, 2, RING)), dma((RING, 2)), dma((2, RING, 2)), dma((2, RING)), dma((2, RING)),
+            dma((RING,)), dma((2, RING)),
             dma((2, TENSORS)), dma((4, TENSORS)),
             dma((2,)), dma((2 * TENSORS,)), dma((2 * TENSORS,)), dma((4,)),
             dma((RING,)), dma((RING,)), dma((2 * RING,)), dma((2 * RING,)),

time: 90.9 us -> 88.6 us (0.975)
  Pallas kernels: 83.8 us -> 81.5 us
    pallas_call x1, Pallas kernels: 83.8 us -> 81.5 us  [head(): pl.pallas_call(head_kernel, out_shape=jax.ShapeDtypeStruct((2 * RING, RIN...]
where the time goes in v5:
time: 88.6 us; the launch traced here: 88.3 us
  Pallas kernels  81.5 us (92%)
  local copies, waits for them, and re-layouts  3.94 us (4%)
  other arithmetic  1.45 us (2%)
  between operations  1.41 us (2%)
    pallas_call x1, Pallas kernels, head(): pl.pallas_call(head_kernel, out_shape=jax.ShapeDtypeStruct((2 * RING, RIN...  81.5 us

profile of v5, /device:TPU:1, one launch (start us, length us, event | category | flops | bytes accessed | tf_op | source)
XLA Modules:
  0.0 88.3 jit_solution(17734205937023498984)
XLA Ops:
  0.6 0.0 copy-start.1
  1.3 0.7 select_add_fusion
  2.1 0.7 fusion.6
  2.8 0.7 slice.16
  3.5 0.1 copy.11.place_ref
  3.7 0.0 copy-done.1
  3.7 0.0 copy-start.2
  3.7 0.1 copy.9
  3.8 0.5 copy-done.2
  4.4 0.0 copy-start
  4.4 0.2 copy.10.gain_ref
  4.6 0.7 copy-done
  5.3 81.5 %shard_map.77 = f32[16,8,128]{2,1,0:T(8,128)S(1)} custom-call(bf16[50,1024]{1,0:T(8,128)(2,1)S(1)} %bitcast.11, bf16[16,128]{1,0:T(8,128)(2,1)S(1)} %reshape.33.rest_hbm, bf16[256,512]{1,0:T(8,128)(2,1)S(1)} %bitcast.9, s32[1,512]{1,0:T(1,128)S(1)} %bitcast.12, f32[1024,1]{1,0:T(8,128)S(1)} %copy.10.gain_ref, s32[512,1]{1,0:T(8,128)S(1)} %copy.11.place_ref, ...), custom_call_target="tpu_custom_call" | custom-call | tf_op jit(solution)/shard_map/pallas_call | solution.py:376
  86.8 0.1 fusion.16
  86.9 0.7 reshape.38
  87.7 0.7 reshape.37
  (5 shorter events, 0.1 us)
Async XLA Ops:
  0.6 3.0 %copy-start.1 = (bf16[512,256]{1,0:T(8,128)(2,1)S(1)}, bf16[512,256]{1,0:T(8,128)(2,1)}, u32[]{:S(2)}) copy-start(bf16[512,256]{1,0:T(8,128)(2,1)} %param.6) | copy-start | bytes 786436
  3.7 0.7 copy-start.2
  4.4 0.9 %copy-start = (bf16[1024,50]{0,1:T(8,128)(2,1)S(1)}, bf16[1024,50]{0,1:T(8,128)(2,1)}, u32[]{:S(2)}) copy-start(bf16[1024,50]{0,1:T(8,128)(2,1)} %param.8) | copy-start | bytes 307204

commit v6 on v5

--- a/solution.py
+++ b/solution.py
@@ -18,9 +18,9 @@
     return ((i + 1) >> 1) * (1 - 2 * (i & 1))
 
 
-def head_kernel(main_hbm, rest_hbm, hid_hbm, code_hbm, gain_ref, place_ref, live_ref, out_ref,
+def head_kernel(main_hbm, rest_hbm, hid_hbm, gain_row, notes, out_ref,
                 wbuf, lbuf, hbuf, cbuf, normed, wide_rest, rest, stats, packed, gath,
-                select, values, line_out, line_in, plane_out, plane_in,
+                gain_ref, select, values, line_out, line_in, plane_out, plane_in,
                 b_recv, b_send, m_recv, m_send, o_recv, o_send, r_recv, r_send, h_recv, h_send, c_sem, s_recv, s_send, local_sem,
                 l_recv, l_send, p_recv, p_send):
     z, y = lax.axis_index("z"), lax.axis_index("y")
@@ -48,10 +48,11 @@
         pltpu.make_async_copy(main_hbm.at[pl.ds(0, MAIN)], wbuf.at[slot0], local_sem.at[0]),
         pltpu.make_async_copy(rest_hbm, lbuf.at[slot0], local_sem.at[1]),
         pltpu.make_async_copy(hid_hbm, hbuf.at[core, x], local_sem.at[2]),
-        pltpu.make_async_copy(code_hbm, cbuf.at[core], local_sem.at[3]),
     ]
     for copy in locals_:
         copy.start()
+    cbuf[core] = notes[pl.ds(0, 1), :]
+    gain_ref[...] = jnp.broadcast_to(gain_row[...], (128, gain_row.shape[1])).T
     barrier = pltpu.get_barrier_semaphore()
     peers = [at_x(x + d, c) for d in range(TENSORS) for c in (core, 1 - core)][1:]
     for peer in [right1, left1, right2, left2] + peers:
@@ -164,7 +165,8 @@
     states(core, x + 2, 3, partner).start()
     second(1, 0)
     spots = lax.broadcasted_iota(jnp.int32, select.shape, 1)
-    select[...] = jnp.where(spots == place_ref[...], 1.0, 0.0).astype(jnp.bfloat16)
+    places = jnp.broadcast_to(notes[pl.ds(1, 1), :].astype(F32), (128, rows)).T
+    select[...] = jnp.where(spots == places[:, :1].astype(jnp.int32), 1.0, 0.0).astype(jnp.bfloat16)
     line_out[...] = jnp.zeros(line_out.shape, F32)
     second(1, 1)
 
@@ -179,7 +181,7 @@
         scale = lax.rsqrt(power / (TENSORS * feats) + 1e-06)
         for d in range(TENSORS):
             span = pl.ds(d * feats, feats)
-            part = hbuf[c, d].astype(F32) * scale * gain_ref[span, :]
+            part = hbuf[c, d].astype(F32) * scale * gain_ref[span, :1]
             normed[span, pl.ds(c * rows, rows)] = part.astype(jnp.bfloat16)
     stats[0] = jnp.full(stats.shape[1:], -1e30, F32)
     for n in range(1, 4):
@@ -279,7 +281,7 @@
     mass = jnp.sum(gath[:, 1, :] * factor, axis=0, keepdims=True)
     moment = jnp.sum(gath[:, 2, :] * factor, axis=0, keepdims=True)
     picked = jnp.sum(gath[:, 3, :], axis=0, keepdims=True)
-    live = live_ref[...] > 0
+    live = notes[pl.ds(2, 1), :] > 0
     lse = top + jnp.log(mass)
     values[pl.ds(0, 1), :] = jnp.where(live, picked - lse, 0.0)
     values[pl.ds(1, 1), :] = jnp.where(live, lse - moment / mass, 0.0)
@@ -367,7 +369,7 @@
     out_ref[...] = plane_in[...]
 
 
-def head(main, rest, hid, code, gain, place, live):
+def head(main, rest, hid, gain, notes):
     rows, feats, slots = hid.shape[1], hid.shape[0], RING * RING
     depth = TENSORS * feats
     any_space = pl.BlockSpec(memory_space=pl.ANY)
@@ -376,7 +378,7 @@
     return pl.pallas_call(
         head_kernel,
         out_shape=jax.ShapeDtypeStruct((2 * RING, RING, 128), F32),
-        in_specs=[any_space] * 4 + [vmem] * 3,
+        in_specs=[any_space] * 3 + [vmem] * 2,
         out_specs=vmem,
         scratch_shapes=[
             pltpu.VMEM((slots, MAIN, depth), jnp.bfloat16),
@@ -389,6 +391,7 @@
             pltpu.VMEM((4, 8, 2 * rows), F32),
             pltpu.VMEM((2, 8, rows), F32),
             pltpu.VMEM((2 * TENSORS, 8, rows), F32),
+            pltpu.VMEM((depth, 128), F32),
             pltpu.VMEM((rows, RING * 128), jnp.bfloat16),
             pltpu.VMEM((2, rows), F32),
             pltpu.VMEM((RING, 8, 128), F32),
@@ -403,7 +406,7 @@
         ],
         compiler_params=pltpu.CompilerParams(
             collective_id=0, has_side_effects=True, vmem_limit_bytes=48 << 20),
-    )(main, rest, hid, code, gain, place, live)
+    )(main, rest, hid, gain, notes)
 
 
 def body(hidden, gain, head_weight, targets, row_count, dest):
@@ -421,13 +424,14 @@
     order = jnp.where(gone < RING // 2, 2 * gone, 2 * (RING - gone) - 1)
     slot = jnp.where(near == 0, yi, zi) * RING + order
     index = jnp.where(column < MAIN, slot * MAIN + column, RING * RING * MAIN + slot * 2 + column - MAIN)
-    code = ((owner * 2 + near) * 4096 + index).reshape(1, rows)
+    code = ((owner * 2 + near) * 4096 + index)
     share = rows // groups
     rank = (dest // rows) * share + dest % share
     line = rows // RING
     place = (rank // line) * 128 + rank % line
     live = (jnp.arange(rows, dtype=jnp.int32) < row_count[0]).astype(jnp.int32)
-    got = head(turned, rest, hidden.T, code, gain.reshape(-1, 1), place.reshape(-1, 1), live.reshape(1, -1))
+    notes = jnp.stack([code, place, live])
+    got = head(turned, rest, hidden.T, gain.reshape(1, -1), notes)
     got = jnp.moveaxis(got[:, :, :2 * share], 1, 0)
     return got[:, :, :share].reshape(rows), got[:, :, share:].reshape(rows)
 

time: 88.6 us -> 88.1 us (level)
  other arithmetic: 1.45 us -> 0.1 us
    unnamed x7 -> x9, local copies, waits for them, and re-layouts: 1.35 us -> 2.47 us
where the time goes in v6:
time: 88.1 us; the launch traced here: 87.9 us
  Pallas kernels  81.7 us (93%)
  local copies, waits for them, and re-layouts  4.7 us (5%)
  between operations  1.37 us (2%)
    pallas_call x1, Pallas kernels, head(): pl.pallas_call(head_kernel, out_shape=jax.ShapeDtypeStruct((2 * RING, RIN...  81.7 us
    unnamed x9, local copies, waits for them, and re-layouts  2.47 us

profile of v6, /device:TPU:1, one launch (start us, length us, event | category | flops | bytes accessed | tf_op | source)
XLA Modules:
  0.0 87.9 jit_solution(7596633518018948817)
XLA Ops:
  1.3 0.0 copy-start.2
  1.3 0.7 copy-done.2
  2.0 0.1 select_add_fusion
  2.0 0.0 copy-start.3
  2.0 0.7 copy-done.3
  2.7 0.7 slice.16
  3.5 0.0 copy-start
  3.5 0.0 copy-start.1
  3.5 1.1 %copy.9 = bf16[512,256]{0,1:T(8,128)(2,1)S(1)} copy(bf16[512,256]{1,0:T(8,128)(2,1)} %param.6) | data formatting | bytes 524288 | tf_op args[0]
  4.6 0.0 copy-done
  4.6 0.0 copy-done.1
  4.7 81.7 %shard_map.77 = f32[16,8,128]{2,1,0:T(8,128)S(1)} custom-call(bf16[50,1024]{1,0:T(8,128)(2,1)S(1)} %bitcast.11, bf16[16,128]{1,0:T(8,128)(2,1)S(1)} %reshape.26.rest_hbm, bf16[256,512]{1,0:T(8,128)(2,1)S(1)} %bitcast.9, f32[1,1024]{1,0:T(1,128)S(1)} %bitcast.12, s32[3,512]{1,0:T(4,128)S(1)} %pad_add_fusion.notes), custom_call_target="tpu_custom_call" | custom-call | tf_op jit(solution)/shard_map/pallas_call | solution.py:378
  86.4 0.1 fusion.16
  86.5 0.7 reshape.29
  87.2 0.7 reshape.28
  (7 shorter events, 0.1 us)
Async XLA Ops:
  1.3 0.7 copy-start.2
  2.0 0.7 copy-start.3
  3.5 1.2 %copy-start = (bf16[1024,50]{0,1:T(8,128)(2,1)S(1)}, bf16[1024,50]{0,1:T(8,128)(2,1)}, u32[]{:S(2)}) copy-start(bf16[1024,50]{0,1:T(8,128)(2,1)} %param.8) | copy-start | bytes 307204
  3.5 1.2 %copy-start.1 = (f32[1024]{0:T(1024)S(1)}, f32[1024]{0:T(1024)}, u32[]{:S(2)}) copy-start(f32[1024]{0:T(1024)} %param.7) | copy-start | bytes 12292
